TPU v7x, 32 devices: a whole 2x2x4 slice. The times are simulated.
32 devices in a mesh: leaf: 4 (over y, x), row: 8 (over z, core).
Axes of the slice: x: 2, y: 2, z: 4, core: 2. Of those that a mesh axis runs over, the one named last changes fastest.
Arguments:
- rhs: bfloat16 [6, 4, 512, 256], P(None, 'leaf', 'row'), may hold values from -6 to 6
- diag_inverse: bfloat16 [4, 6, 512, 512], P('leaf'), as said below
- factor: bfloat16 [4, 58, 512, 512], P('leaf', None, 'row'), as said below
- widths: int32 [6, 4], P(None, 'leaf'), may hold values from 64 to 512, as said below
- structure: int32 [4, 58], P('leaf'), may hold values from 0 to 1, as said below
Outputs:
- forward_solution: bfloat16 [6, 4, 512, 256], P(None, 'leaf', 'row')
- adjoint_solution: bfloat16 [6, 4, 512, 256], P(None, 'leaf', 'row')
Inputs may be any that keep to these rules, and one draw needn't show every extreme that they name: `widths`: every draw has a supernode of exactly 512 columns and one of exactly one eighth of 512 columns. `structure`: 1 where the block is present. Each diag_inverse[j, l] is lower triangular with diagonal entries from 0.5 to 1. `factor`: dense blocks of independent entries.
All inputs are finite; a program needn't handle non-finite values.
Results may differ from a plain program's by a relative error of at most 0.017.
Values may be sent and summed in bfloat16 or wider, within the bound.
No kernel may reach another device: no remote copies, remote signals or barrier semaphores. Data moves between devices by JAX's collectives and lax.ppermute only.
A program may use at most 64 MiB of HBM per device.

v0:
```python
import jax
import jax.numpy as jnp
from jax import lax
from jax.sharding import PartitionSpec as P


def from_partner(x, axis, stride):
    return lax.ppermute(x, axis, [(i, i ^ 1 << stride) for i in range(lax.axis_size(axis))])


def group_size(level_now, leaf_count):
    return min(2**level_now, leaf_count)


def block_offsets(levels, leaf_count):
    offset_table = {}
    cursor = 0
    for source_level in range(levels):
        for target_level in range(source_level + 1, levels):
            offset_table[source_level, target_level] = cursor
            cursor += group_size(target_level, leaf_count)
    return offset_table


def blocks_after(level_now, levels, leaf_count):
    return sum(
        (group_size(target_level, leaf_count) for target_level in range(level_now + 1, levels))
    )


def contract_rows(left_side, right_side):
    return lax.dot_general(
        left_side, right_side, (((0,), (0,)), ((), ())), preferred_element_type=jnp.float32
    )


def apply_columns(matrix, shard_piece):
    return jnp.dot(matrix, shard_piece, preferred_element_type=jnp.float32)


def group_reduce(partials, group_span, leaf_index):
    current = partials
    for bit_number in reversed(range(group_span.bit_length() - 1)):
        half_size = current.shape[0] // 2
        upper_bit = leaf_index // 2**bit_number % 2 == 1
        kept_half = jnp.where(upper_bit, current[half_size:], current[:half_size])
        handed = jnp.where(upper_bit, current[:half_size], current[half_size:])
        current = kept_half + from_partner(handed.astype(jnp.bfloat16), "leaf", bit_number).astype(
            handed.dtype
        )
    return current[0]


def group_collect(own_block, group_span, leaf_index):
    current = own_block[None]
    for bit_number in range(group_span.bit_length() - 1):
        partner = from_partner(current, "leaf", bit_number)
        upper_bit = leaf_index // 2**bit_number % 2 == 1
        current = jnp.where(
            upper_bit,
            jnp.concatenate([partner, current], 0),
            jnp.concatenate([current, partner], 0),
        )
    return current


def adjoint_level(flat_blocks, flat_values, own_full, full_mask, block_mask, inverse_cols):
    pulled = lax.psum(contract_rows(flat_blocks, flat_values).astype(jnp.bfloat16), "row").astype(
        jnp.float32
    )
    reduced_full = (full_mask[:, None] * (own_full.astype(jnp.float32) - pulled)).astype(
        jnp.bfloat16
    )
    solved = contract_rows(inverse_cols, reduced_full)
    return (block_mask[:, None] * solved).astype(jnp.bfloat16)


def shards(rhs, diag_inverse, factor, widths, structure):
    leaf_count = lax.axis_size("leaf")
    leaf_index = lax.axis_index("leaf")
    row_index = lax.axis_index("row")
    levels = rhs.shape[0]
    block_rows = rhs.shape[2]
    columns = rhs.shape[3]
    full_width = factor.shape[3]
    inverse = diag_inverse[0]
    blocks = factor[0]
    weights = structure[0].astype(jnp.float32)
    own_rows = row_index * block_rows
    positions = jnp.arange(full_width, dtype=jnp.int32)
    full_masks = (positions[None, :] < widths).astype(jnp.float32)
    block_masks = lax.dynamic_slice_in_dim(full_masks, own_rows, block_rows, 1)
    offset_table = block_offsets(levels, leaf_count)
    pending = {}
    for target_level in range(1, levels):
        pending[target_level] = jnp.zeros(
            (group_size(target_level, leaf_count), block_rows, columns), jnp.float32
        )
    forward_blocks = []
    forward_full = []
    for level_now in range(levels):
        if level_now > 0:
            incoming = group_reduce(
                pending[level_now], group_size(level_now, leaf_count), leaf_index
            )
        else:
            incoming = jnp.zeros((block_rows, columns), jnp.float32)
        residual = (
            block_masks[level_now][:, None] * (rhs[level_now, 0].astype(jnp.float32) - incoming)
        ).astype(jnp.bfloat16)
        solve_rows = inverse[level_now]
        folded = apply_columns(solve_rows, lax.all_gather(residual, "row", axis=0, tiled=True))
        solved_full = (full_masks[level_now][:, None] * folded).astype(jnp.bfloat16)
        solved_block = lax.dynamic_slice_in_dim(solved_full, own_rows, block_rows, 0)
        forward_blocks.append(solved_block)
        forward_full.append(solved_full)
        if level_now + 1 < levels:
            first_block = offset_table[level_now, level_now + 1]
            block_count = blocks_after(level_now, levels, leaf_count)
            chosen = blocks[first_block : first_block + block_count].reshape(
                block_count * block_rows, full_width
            )
            products = jnp.dot(chosen, solved_full, preferred_element_type=jnp.float32).reshape(
                block_count, block_rows, columns
            )
            products = products * weights[first_block : first_block + block_count][:, None, None]
            cursor = 0
            for target_level in range(level_now + 1, levels):
                group_span = group_size(target_level, leaf_count)
                pending[target_level] = (
                    pending[target_level] + products[cursor : cursor + group_span]
                )
                cursor += group_span
    gathered = {}
    adjoint_blocks = [None] * levels
    for level_now in reversed(range(levels)):
        inverse_cols = lax.dynamic_slice_in_dim(inverse[level_now], own_rows, block_rows, 1)
        if level_now + 1 == levels:
            solved = contract_rows(inverse_cols, forward_full[level_now])
            own_adjoint = (block_masks[level_now][:, None] * solved).astype(jnp.bfloat16)
        else:
            first_block = offset_table[level_now, level_now + 1]
            block_count = blocks_after(level_now, levels, leaf_count)
            stacked = jnp.concatenate(
                [gathered[upper_level] for upper_level in range(level_now + 1, levels)], 0
            )
            stacked = stacked * structure[0, first_block : first_block + block_count][
                :, None, None
            ].astype(jnp.bfloat16)
            flat_blocks = blocks[first_block : first_block + block_count].reshape(
                block_count * block_rows, full_width
            )
            flat_values = stacked.reshape(block_count * block_rows, columns)
            own_adjoint = adjoint_level(
                flat_blocks,
                flat_values,
                forward_full[level_now],
                full_masks[level_now],
                block_masks[level_now],
                inverse_cols,
            )
        adjoint_blocks[level_now] = own_adjoint
        if level_now > 0:
            gathered[level_now] = group_collect(
                own_adjoint, group_size(level_now, leaf_count), leaf_index
            )
    return (jnp.stack(forward_blocks)[:, None], jnp.stack(adjoint_blocks)[:, None])


def solution(mesh):
    placed = (
        P(None, "leaf", "row", None),
        P("leaf", None, None, None),
        P("leaf", None, "row", None),
        P(None, "leaf"),
        P("leaf", None),
    )
    return jax.shard_map(
        shards,
        mesh=mesh,
        in_specs=placed,
        out_specs=(P(None, "leaf", "row", None), P(None, "leaf", "row", None)),
        check_vma=False,
    )
```

profile of v0, /device:TPU:0, one launch (start us, length us, event | category | flops | bytes accessed | tf_op | source)
XLA Modules:
  0.0 502.9 jit_solution(18401244926935718520)
XLA Ops:
  10.1 15.9 %all_gather.18 = bf16[512,256]{1,0:T(8,128)(2,1)S(1)} all-gather(bf16[64,256]{1,0:T(8,128)(2,1)S(1)} %fusion.74), channel_id=1, replica_groups=mesh['leaf'=4,'row'=8] {'row'}, dimensions={0}, use_global_device_ids=true | all-gather | bytes 294912 | tf_op jit(solution)/shard_map/all_gather | solution.py:112
  36.7 14.3 %all_gather.19 = bf16[512,256]{1,0:T(8,128)(2,1)S(1)} all-gather(bf16[64,256]{1,0:T(8,128)(2,1)S(1)} %fusion.73), channel_id=1, replica_groups=mesh['leaf'=4,'row'=8] {'row'}, dimensions={0}, use_global_device_ids=true | all-gather | bytes 294912 | tf_op jit(solution)/shard_map/all_gather | solution.py:112
  54.6 2.5 copy.14
  60.2 2.8 collective-permute-done.1
  67.9 14.2 %all_gather.20 = bf16[512,256]{1,0:T(8,128)(2,1)S(1)} all-gather(bf16[64,256]{1,0:T(8,128)(2,1)S(1)} %fusion.71), channel_id=1, replica_groups=mesh['leaf'=4,'row'=8] {'row'}, dimensions={0}, use_global_device_ids=true | all-gather | bytes 294912 | tf_op jit(solution)/shard_map/all_gather | solution.py:112
  85.5 2.3 copy.15
  90.7 2.8 collective-permute-done.3
  98.4 14.3 %all_gather.21 = bf16[512,256]{1,0:T(8,128)(2,1)S(1)} all-gather(bf16[64,256]{1,0:T(8,128)(2,1)S(1)} %fusion.69), channel_id=1, replica_groups=mesh['leaf'=4,'row'=8] {'row'}, dimensions={0}, use_global_device_ids=true | all-gather | bytes 294912 | tf_op jit(solution)/shard_map/all_gather | solution.py:112
  121.1 2.8 collective-permute-done.5
  128.8 14.2 %all_gather.22 = bf16[512,256]{1,0:T(8,128)(2,1)S(1)} all-gather(bf16[64,256]{1,0:T(8,128)(2,1)S(1)} %fusion.67), channel_id=1, replica_groups=mesh['leaf'=4,'row'=8] {'row'}, dimensions={0}, use_global_device_ids=true | all-gather | bytes 294912 | tf_op jit(solution)/shard_map/all_gather | solution.py:112
  147.5 2.7 collective-permute-done.7
  155.2 14.3 %all_gather.23 = bf16[512,256]{1,0:T(8,128)(2,1)S(1)} all-gather(bf16[64,256]{1,0:T(8,128)(2,1)S(1)} %fusion.65), channel_id=1, replica_groups=mesh['leaf'=4,'row'=8] {'row'}, dimensions={0}, use_global_device_ids=true | all-gather | bytes 294912 | tf_op jit(solution)/shard_map/all_gather | solution.py:112
  171.7 2.4 collective-permute-done.9
  175.9 2.6 collective-permute-done.10
  179.6 56.5 %all-reduce.6.cloned.1.call-done = bf16[512,256]{0,1:T(8,128)(2,1)} async-done(((bf16[512,256]{0,1:T(8,128)(2,1)}), bf16[512,256]{0,1:T(8,128)(2,1)}) %all-reduce.6.cloned.1.call-update) | async-done | bytes 262160 | tf_op jit(solution)/shard_map/psum | solution.py:68
  239.0 2.4 collective-permute-done.11
  243.0 2.7 collective-permute-done.12
  247.0 54.6 %all-reduce.8.cloned.1.call-done = bf16[512,256]{0,1:T(8,128)(2,1)} async-done(((bf16[512,256]{0,1:T(8,128)(2,1)}), bf16[512,256]{0,1:T(8,128)(2,1)}) %all-reduce.8.cloned.1.call-update) | async-done | bytes 262160 | tf_op jit(solution)/shard_map/psum | solution.py:68
  304.5 2.4 collective-permute-done.13
  308.5 2.7 collective-permute-done.14
  312.6 54.5 %all-reduce.10.cloned.1.call-done = bf16[512,256]{0,1:T(8,128)(2,1)} async-done(((bf16[512,256]{0,1:T(8,128)(2,1)}), bf16[512,256]{0,1:T(8,128)(2,1)}) %all-reduce.10.cloned.1.call-update) | async-done | bytes 262160 | tf_op jit(solution)/shard_map/psum | solution.py:68
  370.0 2.4 collective-permute-done.15
  379.6 53.1 %all-reduce.12.cloned.1.call-done = bf16[512,256]{0,1:T(8,128)(2,1)} async-done(((bf16[512,256]{0,1:T(8,128)(2,1)}), bf16[512,256]{0,1:T(8,128)(2,1)}) %all-reduce.12.cloned.1.call-update) | async-done | bytes 262160 | tf_op jit(solution)/shard_map/psum | solution.py:68
  442.4 51.9 %all-reduce.14.cloned.1.call-done = bf16[512,256]{0,1:T(8,128)(2,1)} async-done(((bf16[512,256]{0,1:T(8,128)(2,1)}), bf16[512,256]{0,1:T(8,128)(2,1)}) %all-reduce.14.cloned.1.call-update) | async-done | bytes 262160 | tf_op jit(solution)/shard_map/psum | solution.py:68
  (220 shorter events, 96.6 us)
Async XLA Ops:
  7.2 229.0 %all-reduce.6.cloned.1.call-start = ((), (), s32[]{:S(2)}) async-start(), calls=%async_computation | async-start | bytes 524288 | tf_op jit(solution)/shard_map/psum | solution.py:68
  31.9 4.0 collective-permute-start
  58.6 4.4 collective-permute-start.1
  63.1 4.0 collective-permute-start.2
  89.1 4.4 collective-permute-start.3
  93.6 4.0 collective-permute-start.4
  119.5 4.4 collective-permute-start.5
  123.9 4.0 collective-permute-start.6
  144.5 91.6 %copy-start.14 = (bf16[256,512]{1,0:T(8,128)(2,1)}, bf16[256,512]{1,0:T(8,128)(2,1)S(1)}, u32[]{:S(2)}) copy-start(bf16[256,512]{1,0:T(8,128)(2,1)S(1)} %fusion.4) | copy-start | bytes 786436
  145.9 4.4 collective-permute-start.7
  150.4 4.0 collective-permute-start.8
  170.2 4.0 collective-permute-start.9
  174.2 4.3 collective-permute-start.10
  179.6 122.0 %all-reduce.8.cloned.1.call-start = ((), (), s32[]{:S(2)}) async-start(), calls=%async_computation.1 | async-start | bytes 524288 | tf_op jit(solution)/shard_map/psum | solution.py:68
  237.4 4.0 collective-permute-start.11
  241.4 4.3 collective-permute-start.12
  247.0 120.2 %all-reduce.10.cloned.1.call-start = ((), (), s32[]{:S(2)}) async-start(), calls=%async_computation.2 | async-start | bytes 524288 | tf_op jit(solution)/shard_map/psum | solution.py:68
  302.9 4.0 collective-permute-start.13
  306.9 4.3 collective-permute-start.14
  312.5 120.3 %all-reduce.12.cloned.1.call-start = ((), (), s32[]{:S(2)}) async-start(), calls=%async_computation.3 | async-start | bytes 524288 | tf_op jit(solution)/shard_map/psum | solution.py:68
  368.5 4.0 collective-permute-start.15
  372.5 4.3 collective-permute-start.16
  378.2 116.1 %all-reduce.14.cloned.1.call-start = ((), (), s32[]{:S(2)}) async-start(), calls=%async_computation.4 | async-start | bytes 524288 | tf_op jit(solution)/shard_map/psum | solution.py:68
  434.1 4.0 collective-permute-start.17
  (41 other events, 1000.0 us)
Sparse Core Ops, SparseCore 0:
  179.7 56.4 all-reduce.5
  247.1 54.4 all-reduce.7
  312.6 54.4 all-reduce.9
  378.3 54.4 all-reduce.11
  439.8 54.4 all-reduce.13
where the time goes:
time: 504 us; the launch traced here: 503 us
  waiting for transfers between devices  308 us (61%)
  blocking collectives  87.2 us (17%)
  starting transfers between devices  28.5 us (6%)
  local copies, waits for them, and re-layouts  26.8 us (5%)
  matrix products  24.5 us (5%)
  between operations  14.7 us (3%)
  other arithmetic  12.9 us (3%)
    psum x5, waiting for transfers between devices, adjoint_level(): lax.psum(contract_rows(flat_blocks, flat_values).astype(jnp.bfloat16), 'r...  271 us
    all_gather x6, blocking collectives, shards(): lax.all_gather(residual, 'row', axis=0, tiled=True)  87.2 us
    ppermute x18, waiting for transfers between devices, from_partner(): lax.ppermute(x, axis, [(i, i ^ 1 << stride) for i in range(lax.axis_size(...  37.7 us
    ppermute x18, starting transfers between devices, from_partner(): lax.ppermute(x, axis, [(i, i ^ 1 << stride) for i in range(lax.axis_size(...  28.2 us
    dot_general x11, matrix products, contract_rows(): lax.dot_general(left_side, right_side, (((0,), (0,)), ((), ())), preferre...  12.3 us
    unnamed x97, local copies, waits for them, and re-layouts  10.3 us
  transfers between devices with their start and end apart: 23, of which 23 were waited for; matrix products, arithmetic and copies ran while one was open for 3% of the time, Pallas kernels for 0%

commit v1 on v0

--- a/solution.py
+++ b/solution.py
@@ -65,9 +65,9 @@
 
 
 def adjoint_level(flat_blocks, flat_values, own_full, full_mask, block_mask, inverse_cols):
-    pulled = lax.psum(contract_rows(flat_blocks, flat_values).astype(jnp.bfloat16), "row").astype(
-        jnp.float32
-    )
+    pulled = jnp.sum(
+        lax.all_gather(contract_rows(flat_blocks, flat_values).astype(jnp.bfloat16), "row"), axis=0
+    ).astype(jnp.float32)
     reduced_full = (full_mask[:, None] * (own_full.astype(jnp.float32) - pulled)).astype(
         jnp.bfloat16
     )

time: 504 us -> 393 us (0.78)
  waiting for transfers between devices: 308 us -> 183 us
  other arithmetic: 12.9 us -> 21.6 us
  local copies, waits for them, and re-layouts: 26.8 us -> 34.2 us
    psum x5 -> x0, waiting for transfers between devices: 271 us -> none  [adjoint_level(): lax.psum(contract_rows(flat_blocks, flat_values).astype(jnp.bfloat16), 'r...]
    all_gather x0 -> x5, waiting for transfers between devices: none -> 143 us  [adjoint_level(): lax.all_gather(contract_rows(flat_blocks, flat_values).astype(jnp.bfloat1...]
    reduce_sum x0 -> x5, other arithmetic: none -> 7.77 us  [adjoint_level(): jnp.sum(lax.all_gather(contract_rows(flat_blocks, flat_values).astype(jnp...]
    unnamed x97 -> x78, local copies, waits for them, and re-layouts: 10.3 us -> 17.9 us
  transfers between devices with their start and end apart: 23 -> 23, of which waited for: 23 -> 23; matrix products, arithmetic and copies ran while one was open for 3% -> 2% of each run, Pallas kernels for 0% -> 0%
where the time goes in v1:
time: 393 us; the launch traced here: 391 us
  waiting for transfers between devices  183 us (47%)
  blocking collectives  87.3 us (22%)
  local copies, waits for them, and re-layouts  34.2 us (9%)
  starting transfers between devices  28.5 us (7%)
  matrix products  21.8 us (6%)
  other arithmetic  21.6 us (5%)
  between operations  14.6 us (4%)
    all_gather x5, waiting for transfers between devices, adjoint_level(): lax.all_gather(contract_rows(flat_blocks, flat_values).astype(jnp.bfloat1...  143 us
    all_gather x6, blocking collectives, shards(): lax.all_gather(residual, 'row', axis=0, tiled=True)  87.3 us
    ppermute x18, waiting for transfers between devices, from_partner(): lax.ppermute(x, axis, [(i, i ^ 1 << stride) for i in range(lax.axis_size(...  40.2 us
    ppermute x18, starting transfers between devices, from_partner(): lax.ppermute(x, axis, [(i, i ^ 1 << stride) for i in range(lax.axis_size(...  27.9 us
    unnamed x78, local copies, waits for them, and re-layouts  17.9 us
    dot_general x11, matrix products, contract_rows(): lax.dot_general(left_side, right_side, (((0,), (0,)), ((), ())), preferre...  10.9 us
  transfers between devices with their start and end apart: 23, of which 23 were waited for; matrix products, arithmetic and copies ran while one was open for 2% of the time, Pallas kernels for 0%

profile of v1, /device:TPU:0, one launch (start us, length us, event | category | flops | bytes accessed | tf_op | source)
XLA Modules:
  0.0 391.2 jit_solution(15593401279853406098)
XLA Ops:
  10.1 15.9 %all_gather.48 = bf16[512,256]{1,0:T(8,128)(2,1)S(1)} all-gather(bf16[64,256]{1,0:T(8,128)(2,1)S(1)} %fusion.74), channel_id=1, replica_groups=mesh['leaf'=4,'row'=8] {'row'}, dimensions={0}, use_global_device_ids=true | all-gather | bytes 294912 | tf_op jit(solution)/shard_map/all_gather | solution.py:112
  38.5 14.3 %all_gather.49 = bf16[512,256]{1,0:T(8,128)(2,1)S(1)} all-gather(bf16[64,256]{1,0:T(8,128)(2,1)S(1)} %fusion.73), channel_id=1, replica_groups=mesh['leaf'=4,'row'=8] {'row'}, dimensions={0}, use_global_device_ids=true | all-gather | bytes 294912 | tf_op jit(solution)/shard_map/all_gather | solution.py:112
  56.4 2.5 copy.14
  61.9 2.8 collective-permute-done.1
  69.6 14.2 %all_gather.50 = bf16[512,256]{1,0:T(8,128)(2,1)S(1)} all-gather(bf16[64,256]{1,0:T(8,128)(2,1)S(1)} %fusion.71), channel_id=1, replica_groups=mesh['leaf'=4,'row'=8] {'row'}, dimensions={0}, use_global_device_ids=true | all-gather | bytes 294912 | tf_op jit(solution)/shard_map/all_gather | solution.py:112
  92.5 2.8 collective-permute-done.3
  100.2 14.3 %all_gather.51 = bf16[512,256]{1,0:T(8,128)(2,1)S(1)} all-gather(bf16[64,256]{1,0:T(8,128)(2,1)S(1)} %fusion.69), channel_id=1, replica_groups=mesh['leaf'=4,'row'=8] {'row'}, dimensions={0}, use_global_device_ids=true | all-gather | bytes 294912 | tf_op jit(solution)/shard_map/all_gather | solution.py:112
  121.9 2.8 collective-permute-done.5
  129.6 14.3 %all_gather.52 = bf16[512,256]{1,0:T(8,128)(2,1)S(1)} all-gather(bf16[64,256]{1,0:T(8,128)(2,1)S(1)} %fusion.67), channel_id=1, replica_groups=mesh['leaf'=4,'row'=8] {'row'}, dimensions={0}, use_global_device_ids=true | all-gather | bytes 294912 | tf_op jit(solution)/shard_map/all_gather | solution.py:112
  147.2 2.9 collective-permute-done.7
  155.0 14.3 %all_gather.53 = bf16[512,256]{1,0:T(8,128)(2,1)S(1)} all-gather(bf16[64,256]{1,0:T(8,128)(2,1)S(1)} %fusion.65), channel_id=1, replica_groups=mesh['leaf'=4,'row'=8] {'row'}, dimensions={0}, use_global_device_ids=true | all-gather | bytes 294912 | tf_op jit(solution)/shard_map/all_gather | solution.py:112
  175.5 2.7 collective-permute-done.10
  179.6 30.0 %all-gather.11.cloned.1.call-done = bf16[4096,256]{0,1:T(8,128)(2,1)} async-done(((bf16[512,256]{0,1:T(8,128)(2,1)}), bf16[4096,256]{0,1:T(8,128)(2,1)}) %all-gather.11.cloned.1.call-update) | async-done | bytes 2097168 | tf_op jit(solution)/shard_map/all_gather | solution.py:69
  209.5 2.5 copy.19
  219.5 2.7 collective-permute-done.12
  223.4 28.7 %all-gather.13.cloned.1.call-done = bf16[4096,256]{0,1:T(8,128)(2,1)} async-done(((bf16[512,256]{0,1:T(8,128)(2,1)}), bf16[4096,256]{0,1:T(8,128)(2,1)}) %all-gather.13.cloned.1.call-update) | async-done | bytes 2097168 | tf_op jit(solution)/shard_map/all_gather | solution.py:69
  252.1 2.5 copy.20
  263.0 2.7 collective-permute-done.14
  267.0 28.7 %all-gather.15.cloned.1.call-done = bf16[4096,256]{0,1:T(8,128)(2,1)} async-done(((bf16[512,256]{0,1:T(8,128)(2,1)}), bf16[4096,256]{0,1:T(8,128)(2,1)}) %all-gather.15.cloned.1.call-update) | async-done | bytes 2097168 | tf_op jit(solution)/shard_map/all_gather | solution.py:69
  295.6 2.5 copy.21
  306.5 2.7 collective-permute-done.16
  310.8 28.4 %all-gather.17.cloned.1.call-done = bf16[4096,256]{0,1:T(8,128)(2,1)} async-done(((bf16[512,256]{0,1:T(8,128)(2,1)}), bf16[4096,256]{0,1:T(8,128)(2,1)}) %all-gather.17.cloned.1.call-update) | async-done | bytes 2097168 | tf_op jit(solution)/shard_map/all_gather | solution.py:69
  339.3 2.5 copy.22
  351.5 27.2 %all-gather.19.cloned.1.call-done = bf16[4096,256]{0,1:T(8,128)(2,1)} async-done(((bf16[512,256]{0,1:T(8,128)(2,1)}), bf16[4096,256]{0,1:T(8,128)(2,1)}) %all-gather.19.cloned.1.call-update) | async-done | bytes 2097168 | tf_op jit(solution)/shard_map/all_gather | solution.py:69
  (206 shorter events, 111.7 us)
Async XLA Ops:
  7.2 202.4 %all-gather.11.cloned.1.call-start = ((), (), s32[]{:S(2)}) async-start(), calls=%async_computation | async-start | bytes 2359296 | tf_op jit(solution)/shard_map/all_gather | solution.py:69
  33.7 4.0 %collective-permute-start = (bf16[1,64,256]{2,1,0:T(8,128)(2,1)S(1)}, bf16[1,64,256]{2,1,0:T(8,128)(2,1)S(1)}, u32[]{:S(2)}, u32[]{:S(2)}) collective-permute-start(bf16[1,64,256]{2,1,0:T(8,128)(2,1)S(1)} %select_convert_fusion.8), channel_id=1, source_target_pairs={{0,8},{8,0},{16,24},{24,16},{1,9},{9,1},{17,25},{25,17},{2,10},{10... | collective-permute-start | bytes 98312 | tf_op jit(solution)/shard_map/ppermute | solution.py:8
  60.3 30.5 %copy-start = (f32[16,64,256]{2,1,0:T(8,128)}, f32[16,64,256]{2,1,0:T(8,128)S(1)}, u32[]{:S(2)}) copy-start(f32[16,64,256]{2,1,0:T(8,128)S(1)} %broadcast_multiply_fusion.1) | copy-start | bytes 3145732
  60.4 4.4 %collective-permute-start.1 = (bf16[2,64,256]{2,1,0:T(8,128)(2,1)S(1)}, bf16[2,64,256]{2,1,0:T(8,128)(2,1)S(1)}, u32[]{:S(2)}, u32[]{:S(2)}) collective-permute-start(bf16[2,64,256]{2,1,0:T(8,128)(2,1)S(1)} %select_convert_fusion.3), channel_id=1, source_target_pairs={{0,16},{8,24},{16,0},{24,8},{1,17},{9,25},{17,1},{25,9},{2,18},{10... | collective-permute-start | bytes 196616 | tf_op jit(solution)/shard_map/ppermute | solution.py:8
  64.8 4.0 %collective-permute-start.2 = (bf16[1,64,256]{2,1,0:T(8,128)(2,1)S(1)}, bf16[1,64,256]{2,1,0:T(8,128)(2,1)S(1)}, u32[]{:S(2)}, u32[]{:S(2)}) collective-permute-start(bf16[1,64,256]{2,1,0:T(8,128)(2,1)S(1)} %select_convert_fusion.7), channel_id=1, source_target_pairs={{0,8},{8,0},{16,24},{24,16},{1,9},{9,1},{17,25},{25,17},{2,10},{10... | collective-permute-start | bytes 98312 | tf_op jit(solution)/shard_map/ppermute | solution.py:8
  90.9 4.4 %collective-permute-start.3 = (bf16[2,64,256]{2,1,0:T(8,128)(2,1)S(1)}, bf16[2,64,256]{2,1,0:T(8,128)(2,1)S(1)}, u32[]{:S(2)}, u32[]{:S(2)}) collective-permute-start(bf16[2,64,256]{2,1,0:T(8,128)(2,1)S(1)} %select_convert_fusion.2), channel_id=1, source_target_pairs={{0,16},{8,24},{16,0},{24,8},{1,17},{9,25},{17,1},{25,9},{2,18},{10... | collective-permute-start | bytes 196616 | tf_op jit(solution)/shard_map/ppermute | solution.py:8
  95.3 4.0 %collective-permute-start.4 = (bf16[1,64,256]{2,1,0:T(8,128)(2,1)S(1)}, bf16[1,64,256]{2,1,0:T(8,128)(2,1)S(1)}, u32[]{:S(2)}, u32[]{:S(2)}) collective-permute-start(bf16[1,64,256]{2,1,0:T(8,128)(2,1)S(1)} %select_convert_fusion.6), channel_id=1, source_target_pairs={{0,8},{8,0},{16,24},{24,16},{1,9},{9,1},{17,25},{25,17},{2,10},{10... | collective-permute-start | bytes 98312 | tf_op jit(solution)/shard_map/ppermute | solution.py:8
  120.4 4.4 %collective-permute-start.5 = (bf16[2,64,256]{2,1,0:T(8,128)(2,1)S(1)}, bf16[2,64,256]{2,1,0:T(8,128)(2,1)S(1)}, u32[]{:S(2)}, u32[]{:S(2)}) collective-permute-start(bf16[2,64,256]{2,1,0:T(8,128)(2,1)S(1)} %select_convert_fusion.1), channel_id=1, source_target_pairs={{0,16},{8,24},{16,0},{24,8},{1,17},{9,25},{17,1},{25,9},{2,18},{10... | collective-permute-start | bytes 196616 | tf_op jit(solution)/shard_map/ppermute | solution.py:8
  124.8 4.0 %collective-permute-start.6 = (bf16[1,64,256]{2,1,0:T(8,128)(2,1)S(1)}, bf16[1,64,256]{2,1,0:T(8,128)(2,1)S(1)}, u32[]{:S(2)}, u32[]{:S(2)}) collective-permute-start(bf16[1,64,256]{2,1,0:T(8,128)(2,1)S(1)} %select_convert_fusion.5), channel_id=1, source_target_pairs={{0,8},{8,0},{16,24},{24,16},{1,9},{9,1},{17,25},{25,17},{2,10},{10... | collective-permute-start | bytes 98312 | tf_op jit(solution)/shard_map/ppermute | solution.py:8
  145.7 4.4 %collective-permute-start.7 = (bf16[2,64,256]{2,1,0:T(8,128)(2,1)S(1)}, bf16[2,64,256]{2,1,0:T(8,128)(2,1)S(1)}, u32[]{:S(2)}, u32[]{:S(2)}) collective-permute-start(bf16[2,64,256]{2,1,0:T(8,128)(2,1)S(1)} %select_convert_fusion), channel_id=1, source_target_pairs={{0,16},{8,24},{16,0},{24,8},{1,17},{9,25},{17,1},{25,9},{2,18},{10... | collective-permute-start | bytes 196616 | tf_op jit(solution)/shard_map/ppermute | solution.py:8
  150.2 4.0 %collective-permute-start.8 = (bf16[1,64,256]{2,1,0:T(8,128)(2,1)S(1)}, bf16[1,64,256]{2,1,0:T(8,128)(2,1)S(1)}, u32[]{:S(2)}, u32[]{:S(2)}) collective-permute-start(bf16[1,64,256]{2,1,0:T(8,128)(2,1)S(1)} %select_convert_fusion.4), channel_id=1, source_target_pairs={{0,8},{8,0},{16,24},{24,16},{1,9},{9,1},{17,25},{25,17},{2,10},{10... | collective-permute-start | bytes 98312 | tf_op jit(solution)/shard_map/ppermute | solution.py:8
  169.9 4.0 %collective-permute-start.9 = (bf16[1,64,256]{2,1,0:T(8,128)(2,1)S(1)}, bf16[1,64,256]{2,1,0:T(8,128)(2,1)S(1)}, u32[]{:S(2)}, u32[]{:S(2)}) collective-permute-start(bf16[1,64,256]{2,1,0:T(8,128)(2,1)S(1)} %fusion.23), channel_id=1, source_target_pairs={{0,8},{8,0},{16,24},{24,16},{1,9},{9,1},{17,25},{25,17},{2,10},{10... | collective-permute-start | bytes 98312 | tf_op jit(solution)/shard_map/ppermute | solution.py:8
  173.9 4.3 %collective-permute-start.10 = (bf16[2,64,256]{2,1,0:T(8,128)(2,1)S(1)}, bf16[2,64,256]{2,1,0:T(8,128)(2,1)S(1)}, u32[]{:S(2)}, u32[]{:S(2)}) collective-permute-start(bf16[2,64,256]{2,1,0:T(8,128)(2,1)S(1)} %maximum_select_fusion.4), channel_id=1, source_target_pairs={{0,16},{8,24},{16,0},{24,8},{1,17},{9,25},{17,1},{25,9},{2,18},{10... | collective-permute-start | bytes 196616 | tf_op jit(solution)/shard_map/ppermute | solution.py:8
  179.3 72.7 %all-gather.13.cloned.1.call-start = ((), (), s32[]{:S(2)}) async-start(), calls=%async_computation.1 | async-start | bytes 2359296 | tf_op jit(solution)/shard_map/all_gather | solution.py:69
  213.9 4.0 %collective-permute-start.11 = (bf16[1,64,256]{2,1,0:T(8,128)(2,1)S(1)}, bf16[1,64,256]{2,1,0:T(8,128)(2,1)S(1)}, u32[]{:S(2)}, u32[]{:S(2)}) collective-permute-start(bf16[1,64,256]{2,1,0:T(8,128)(2,1)S(1)} %fusion.22), channel_id=1, source_target_pairs={{0,8},{8,0},{16,24},{24,16},{1,9},{9,1},{17,25},{25,17},{2,10},{10... | collective-permute-start | bytes 98312 | tf_op jit(solution)/shard_map/ppermute | solution.py:8
  217.9 4.3 %collective-permute-start.12 = (bf16[2,64,256]{2,1,0:T(8,128)(2,1)S(1)}, bf16[2,64,256]{2,1,0:T(8,128)(2,1)S(1)}, u32[]{:S(2)}, u32[]{:S(2)}) collective-permute-start(bf16[2,64,256]{2,1,0:T(8,128)(2,1)S(1)} %maximum_select_fusion.5), channel_id=1, source_target_pairs={{0,16},{8,24},{16,0},{24,8},{1,17},{9,25},{17,1},{25,9},{2,18},{10... | collective-permute-start | bytes 196616 | tf_op jit(solution)/shard_map/ppermute | solution.py:8
  223.4 72.3 %all-gather.15.cloned.1.call-start = ((), (), s32[]{:S(2)}) async-start(), calls=%async_computation.2 | async-start | bytes 2359296 | tf_op jit(solution)/shard_map/all_gather | solution.py:69
  257.4 4.0 %collective-permute-start.13 = (bf16[1,64,256]{2,1,0:T(8,128)(2,1)S(1)}, bf16[1,64,256]{2,1,0:T(8,128)(2,1)S(1)}, u32[]{:S(2)}, u32[]{:S(2)}) collective-permute-start(bf16[1,64,256]{2,1,0:T(8,128)(2,1)S(1)} %fusion.21), channel_id=1, source_target_pairs={{0,8},{8,0},{16,24},{24,16},{1,9},{9,1},{17,25},{25,17},{2,10},{10... | collective-permute-start | bytes 98312 | tf_op jit(solution)/shard_map/ppermute | solution.py:8
  261.4 4.3 %collective-permute-start.14 = (bf16[2,64,256]{2,1,0:T(8,128)(2,1)S(1)}, bf16[2,64,256]{2,1,0:T(8,128)(2,1)S(1)}, u32[]{:S(2)}, u32[]{:S(2)}) collective-permute-start(bf16[2,64,256]{2,1,0:T(8,128)(2,1)S(1)} %maximum_select_fusion.6), channel_id=1, source_target_pairs={{0,16},{8,24},{16,0},{24,8},{1,17},{9,25},{17,1},{25,9},{2,18},{10... | collective-permute-start | bytes 196616 | tf_op jit(solution)/shard_map/ppermute | solution.py:8
  266.9 72.3 %all-gather.17.cloned.1.call-start = ((), (), s32[]{:S(2)}) async-start(), calls=%async_computation.3 | async-start | bytes 2359296 | tf_op jit(solution)/shard_map/all_gather | solution.py:69
  300.9 4.0 %collective-permute-start.15 = (bf16[1,64,256]{2,1,0:T(8,128)(2,1)S(1)}, bf16[1,64,256]{2,1,0:T(8,128)(2,1)S(1)}, u32[]{:S(2)}, u32[]{:S(2)}) collective-permute-start(bf16[1,64,256]{2,1,0:T(8,128)(2,1)S(1)} %fusion.20), channel_id=1, source_target_pairs={{0,8},{8,0},{16,24},{24,16},{1,9},{9,1},{17,25},{25,17},{2,10},{10... | collective-permute-start | bytes 98312 | tf_op jit(solution)/shard_map/ppermute | solution.py:8
  304.9 4.3 %collective-permute-start.16 = (bf16[2,64,256]{2,1,0:T(8,128)(2,1)S(1)}, bf16[2,64,256]{2,1,0:T(8,128)(2,1)S(1)}, u32[]{:S(2)}, u32[]{:S(2)}) collective-permute-start(bf16[2,64,256]{2,1,0:T(8,128)(2,1)S(1)} %maximum_select_fusion.7), channel_id=1, source_target_pairs={{0,16},{8,24},{16,0},{24,8},{1,17},{9,25},{17,1},{25,9},{2,18},{10... | collective-permute-start | bytes 196616 | tf_op jit(solution)/shard_map/ppermute | solution.py:8
  310.6 68.1 %all-gather.19.cloned.1.call-start = ((), (), s32[]{:S(2)}) async-start(), calls=%async_computation.4 | async-start | bytes 2359296 | tf_op jit(solution)/shard_map/all_gather | solution.py:69
  344.5 4.0 %collective-permute-start.17 = (bf16[1,64,256]{2,1,0:T(8,128)(2,1)S(1)}, bf16[1,64,256]{2,1,0:T(8,128)(2,1)S(1)}, u32[]{:S(2)}, u32[]{:S(2)}) collective-permute-start(bf16[1,64,256]{2,1,0:T(8,128)(2,1)S(1)} %fusion.19), channel_id=1, source_target_pairs={{0,8},{8,0},{16,24},{24,16},{1,9},{9,1},{17,25},{25,17},{2,10},{10... | collective-permute-start | bytes 98312 | tf_op jit(solution)/shard_map/ppermute | solution.py:8
  (29 other events, 236.9 us)
Sparse Core Ops, SparseCore 0:
  179.5 30.0 all-gather.10
  223.5 28.5 all-gather.12
  267.0 28.5 all-gather.14
  310.7 28.5 all-gather.16
  350.1 28.5 all-gather.18
